TPU v7x, 32 devices: a whole 2x2x4 slice. The times are simulated.
32 devices in a mesh: gx: 16 (over z, y, x), gy: 2 (over core).
Axes of the slice: x: 2, y: 2, z: 4, core: 2. Of those that a mesh axis runs over, the one named last changes fastest.
Arguments:
- displacement: float32 [3, 32, 128, 256], P(None, None, 'gx', 'gy'), may hold values from -6 to 6
- velocity: float32 [3, 32, 128, 256], P(None, None, 'gx', 'gy'), may hold values from -6 to 6
- slopes: float32 [2, 32, 128, 256], P(None, None, 'gx', 'gy'), may hold values from -0.5 to 0.5
- stretch: float32 [32, 128, 256], P(None, 'gx', 'gy'), may hold values from 0.6 to 1.4
- moduli: float32 [2, 32, 128, 256], P(None, None, 'gx', 'gy'), may hold values from 0.3 to 1
- buoyancy: float32 [32, 128, 256], P(None, 'gx', 'gy'), may hold values from 0.5 to 1.5
- probes: float32 [4, 128, 128], P(None, 'gy'), may hold values from -0.0048828125 to 0.0048828125
Outputs:
- final_displacement: float32 [3, 32, 128, 256], P(None, None, 'gx', 'gy')
- basis: float32 [64, 48, 128], P('gx', 'gy')
- factor: float32 [128, 128], replicated
All inputs are finite; a program needn't handle non-finite values.
Results may differ from a plain program's by a relative error of at most 0.0003.
Values sent between devices are 32-bit elements; how exact they have to be, the bound alone decides.
No kernel may reach another device: no remote copies, remote signals or barrier semaphores. Data moves between devices by JAX's collectives and lax.ppermute only.
A program may use at most 64 MiB of HBM per device.

v0:
```python
import math
from functools import partial

import jax
import jax.numpy as jnp
from jax import lax
from jax.experimental import pallas as pl
from jax.experimental.pallas import tpu as pltpu
from jax.sharding import PartitionSpec as P


STEPS = 4
SUB = 8
AHEAD = 2

time_step = 0.12


def roll(value, shift, axis=-1):
    axis = axis % value.ndim
    shift = shift % value.shape[axis]
    return value if shift == 0 else pltpu.roll(value, shift, axis)


def lanes_of(shape):
    return lax.broadcasted_iota(jnp.int32, shape, len(shape) - 1)


def layer_derivative(value):
    groups = value.shape[0] // SUB
    parts = [value[SUB * v : SUB * (v + 1)] for v in range(groups)]
    sub = lax.broadcasted_iota(jnp.int32, parts[0].shape, 0)
    shifted = {}

    def at(v):
        if 0 <= v < groups:
            return parts[v]
        if v not in shifted:
            if v >= groups:
                shifted[v] = jnp.where(sub < SUB - 1, roll(parts[v - groups], -1, 0), 0.0)
            else:
                shifted[v] = jnp.where(sub > 0, roll(parts[v + groups], 1, 0), 0.0)
        return shifted[v]

    return jnp.concatenate(
        [at(v - 2) - at(v + 2) + 8.0 * (at(v + 1) - at(v - 1)) for v in range(groups)], 0
    )


def band_matrix(count):
    row = lax.broadcasted_iota(jnp.int32, (count, count), 0)
    col = lax.broadcasted_iota(jnp.int32, (count, count), 1)
    away = row - col
    band = jnp.where(
        away == -2,
        1.0,
        jnp.where(away == 2, -1.0, jnp.where(away == 1, 8.0, jnp.where(away == -1, -8.0, 0.0))),
    )
    return band.astype(jnp.bfloat16)


def banded(value, band):
    high = value.astype(jnp.bfloat16)
    low = (value - high.astype(jnp.float32)).astype(jnp.bfloat16)
    return jnp.dot(high, band, preferred_element_type=jnp.float32) + jnp.dot(
        low, band, preferred_element_type=jnp.float32
    )


def edge_terms(edge, window):
    w = lanes_of(edge.shape) % window
    up_2, up_3 = roll(edge, 2), roll(edge, 3)
    down_2, down_3 = roll(edge, -2), roll(edge, -3)
    right = jnp.where(w == 7, 8.0 * up_3, 0.0) - up_2
    left = down_2 - jnp.where(w == 8, 8.0 * down_3, 0.0)
    return jnp.where((w == 6) | (w == 7), right, left)


def edge_spread(terms, place, window):
    count = terms.shape[-1]
    lane = lanes_of(terms.shape)
    return jnp.where((lane < 2) | (lane >= count - 2), roll(terms, count - 2 - window * place - 6), 0.0)


def edge_message(load, x_count, rows, y_count, which=None):
    window = y_count // x_count
    place = lanes_of((rows, y_count)) // window
    message = None
    for x in which or range(x_count):
        moved = roll(load(x), window * x + 4)
        message = moved if message is None else jnp.where(place == x, moved, message)
    return message


def neighbours():
    at = lax.axis_index("gy")
    return (at > 0).astype(jnp.float32), (at < lax.axis_size("gy") - 1).astype(jnp.float32)


def edge_tile(own, from_left, from_right, has_left, has_right, window):
    w = lanes_of(own.shape) % window
    halo = jnp.where(w < 8, from_right * has_right, roll(from_left, 8) * has_left)
    mine = jnp.where(w < 4, own, roll(own, 8))
    return jnp.where((w >= 4) & (w < 12), halo, mine)


def strided(ref, x_count, rows, index=()):
    groups = rows // SUB

    def at(x):
        return jnp.concatenate(
            [
                ref[(*index, pl.ds(x_count * v + x, SUB, stride=groups * x_count), slice(None))]
                for v in range(groups)
            ],
            0,
        )

    return at


def central(far_low, near_low, near_high, far_high):
    def minus(first, second):
        if second is None:
            return first
        return -second if first is None else first - second

    near, far = minus(near_high, near_low), minus(far_low, far_high)
    if near is None:
        return far
    return 8.0 * near if far is None else far + 8.0 * near


def halves(far_ref, near_ref, half):
    def at(c, x):
        return far_ref[c * half + x] if x < half else near_ref[c * half + x - half]

    return at


def is_odd():
    return lax.axis_index("gx") % 2 == 1


def mirrored(values, odd, flip=False):
    other = [-value if flip else value for value in values[::-1]]
    return [jnp.where(odd, second, first) for first, second in zip(values, other)]


class Side:
    def __init__(self, far, x_count):
        self.far, self.half, self.x_count = far, x_count // 2, x_count
        self.inside = range(self.half) if far else range(self.half, x_count)
        self.outside = (-2, -1) if far else (x_count, x_count + 1)

    def depth(self, x):
        return -1 - x if self.far else x - self.x_count

    def at(self, ref, first, index, x, negate, terms=None):
        place = self.depth(x) if self.far else 1 - self.depth(x)
        value = ref[first + 2 * index + place]
        value = -value if negate else value
        return value if terms is None else value + terms

    def halo(self, ref, c, x, terms=None):
        terms = None if terms is None or c > 1 else terms[self.slot(c, x)]
        return self.at(ref, 0, c, x, c == 0, terms)

    def own_part(self, ref, i, x, terms=None):
        return self.at(ref, 6, i, x, i > 0, None if terms is None else terms[self.slot(2 + i, x)])

    def modulus(self, ref, m, x):
        return self.at(ref, 12, m, x, False)

    def slot(self, index, x):
        return 10 * (not self.far) + 2 * index + self.depth(x)

    def packed(self, ref, f, x, window):
        place = 2 * f + (self.depth(x) if self.far else 1 - self.depth(x))
        value = roll(ref[16], ref.shape[2] - 4 - window * place)
        return -value if f == 1 else value

    def pack(self, messages, window):
        place = lanes_of(messages[0].shape) // (2 * window)
        packed = None
        for f, message in enumerate(messages):
            moved = roll(message, window * (2 * f - (0 if self.far else self.x_count - 2)))
            packed = moved if packed is None else jnp.where(place == f, moved, packed)
        return packed

    def send(self, ref, u, metric):
        for k, x in enumerate(self.inside[:2] if self.far else self.inside[-2:]):
            slope_x, slope_y, stretch, lame, shear = (metric(m, x) for m in range(5))
            dr = [layer_derivative(u(c, x)) for c in range(3)]
            near = [x + j if x + j in self.inside else None for j in (-2, -1, 1, 2)]
            dx = [central(*(None if j is None else u(c, j) for j in near)) for c in range(3)]
            g11 = dx[0] + slope_x * dr[0]
            parts = (
                lame * (g11 + slope_y * dr[1] + stretch * dr[2]) + (shear + shear) * g11,
                shear * (slope_y * dr[0] + dx[1] + slope_x * dr[1]),
                shear * (stretch * dr[0] + dx[2] + slope_x * dr[2]),
            )
            for c in range(3):
                ref[2 * c + k] = u(c, x)
                ref[6 + 2 * c + k] = parts[c]


def begin_kernel(*refs):
    sources, held, sems = refs[:5], refs[11:16], refs[16]
    far_ref, near_ref, far_send, near_send, edge_ref, metric_ref = refs[5:11]
    u_ref, slope_ref, stretch_ref, moduli_ref, buoyancy_ref = held
    copies = [
        pltpu.make_async_copy(source, target, sems.at[i])
        for i, (source, target) in enumerate(zip(sources, held))
    ]
    for copy in copies:
        copy.start()
    copies[0].wait()
    x_count, rows, y_count = metric_ref.shape[1:]
    half = x_count // 2
    comps = u_ref.shape[0]
    odd = is_odd()
    for c in range(comps):
        at = strided(u_ref, x_count, rows, (c,))
        slabs = mirrored([at(x) for x in range(x_count)], odd, c == 0)
        for k in range(half):
            far_ref[c * half + k] = slabs[k]
            near_ref[c * half + k] = slabs[half + k]
        edge_ref[c] = edge_message(lambda x: slabs[x], x_count, rows, y_count)
    for copy in copies[1:]:
        copy.wait()
    fields = [
        (strided(slope_ref, x_count, rows, (0,)), None),
        (strided(slope_ref, x_count, rows, (1,)), None),
        (strided(stretch_ref, x_count, rows), None),
        (strided(moduli_ref, x_count, rows, (0,)), 1.0 / 12.0),
        (strided(moduli_ref, x_count, rows, (1,)), 1.0 / 12.0),
    ]
    for m, (at, scale) in enumerate(fields):
        slabs = mirrored([at(x) for x in range(x_count)], odd, m == 0)
        if scale is not None:
            slabs = [slab * scale for slab in slabs]
        for x in range(x_count):
            metric_ref[m, x] = slabs[x]
        for k in range(2):
            if m > 2:
                far_send[6 + 2 * m + k] = slabs[k]
                near_send[6 + 2 * m + k] = slabs[x_count - 2 + k]
        edge_ref[comps + m] = edge_message(lambda x: slabs[x], x_count, rows, y_count)
    at = strided(buoyancy_ref, x_count, rows)
    slabs = mirrored([at(x) for x in range(x_count)], odd)
    push = edge_message(lambda x: slabs[x], x_count, rows, y_count) * (time_step**2 / 12.0)
    u, window = halves(far_ref, near_ref, half), y_count // x_count
    for far, ref in ((True, far_send), (False, near_send)):
        side = Side(far, x_count)
        side.send(ref, u, lambda m, x: metric_ref[m, x])
        ref[16] = side.pack([push, *(edge_ref[comps + m] for m in range(3))], window)


def rest_kernel(u_ref, v_ref, buoyancy_ref, before_far, before_near, push_ref):
    x_count, rows, _ = push_ref.shape
    half = x_count // 2
    odd = is_odd()
    at = strided(buoyancy_ref, x_count, rows)
    for x, value in enumerate(mirrored([at(x) for x in range(x_count)], odd)):
        push_ref[x] = value * (time_step**2 / 12.0)
    for c in range(u_ref.shape[0]):
        at, rate = strided(u_ref, x_count, rows, (c,)), strided(v_ref, x_count, rows, (c,))
        before = [at(x) - time_step * rate(x) for x in range(x_count)]
        for x, value in enumerate(mirrored(before, odd, c == 0)):
            (before_far if x < half else before_near)[c * half + x % half] = value


def corner_kernel(x_count, fixed, far_ref, near_ref, *refs):
    corner_ref, terms = refs[-1], refs[0] if fixed else None
    rows, y_count = far_ref.shape[1:]
    places = {}
    for far, ref in ((True, far_ref), (False, near_ref)):
        side = Side(far, x_count)
        places.update({x % x_count: (side, ref, x) for x in side.outside})

    def load(c, place):
        side, ref, x = places[place]
        return side.halo(ref, c, x, terms) if c < 2 else side.modulus(ref, c - 2, x)

    for c in range(corner_ref.shape[0]):
        corner_ref[c] = edge_message(
            lambda place: load(c, place), x_count, rows, y_count, tuple(places)
        )


def corner_tile(corner_in, c, window, has_left, has_right):
    w = lanes_of(corner_in[0].shape[1:]) % window
    return jnp.where(w < 8, corner_in[-1][c] * has_right, roll(corner_in[0][c], 8) * has_left)


def beyond_change(value, window, x_count):
    place = lanes_of(value.shape) // window

    def near(k):
        inside = (place + k < x_count) if k > 0 else (place + k >= 0)
        return jnp.where(inside, 0.0, roll(value, -window * k))

    return central(*(near(k) for k in (-2, -1, 1, 2)))


def all_stresses(grads, lame, shear):
    pressure = lame * (grads[0][0] + grads[1][1] + grads[2][2])
    twice = shear + shear
    return (
        pressure + twice * grads[0][0],
        pressure + twice * grads[1][1],
        pressure + twice * grads[2][2],
        shear * (grads[0][1] + grads[1][0]),
        shear * (grads[0][2] + grads[2][0]),
        shear * (grads[1][2] + grads[2][1]),
    )


def tile_kernel(sides, comps, *refs):
    low_ref, high_ref, edge_ref = refs[:3]
    edge_in = refs[3 : 3 + sides]
    metric_ref, first_edge = refs[3 + sides : 5 + sides]
    first_edge_in = refs[5 + sides : 5 + 2 * sides]
    s_x, s_o, e_s = refs[5 + 2 * sides :]
    x_count, rows, y_count = metric_ref.shape[1:]
    half, window = x_count // 2, y_count // x_count
    has_left, has_right = neighbours()
    place = lanes_of((rows, y_count)) // window
    u = halves(low_ref, high_ref, half)
    band = band_matrix(y_count)

    edges, across = [], []
    for c in range(comps):
        edge = edge_tile(edge_ref[c], edge_in[0][c], edge_in[-1][c], has_left, has_right, window)
        terms = edge_terms(edge, window)
        result = banded(jnp.concatenate([u(c, x) for x in range(x_count)], 0), band)
        edges.append(edge)
        across.append(
            [
                result[x * rows : (x + 1) * rows] + edge_spread(terms, x, window)
                for x in range(x_count)
            ]
        )

    def gradients(along, beside, layers, metric):
        return [
            [
                along[c] + metric[0] * layers[c],
                beside[c] + metric[1] * layers[c],
                metric[2] * layers[c],
            ]
            for c in range(comps)
        ]

    for x in range(x_count):
        metric = [metric_ref[m, x] for m in range(5)]

        def near(c, k):
            return u(c, x + k) if 0 <= x + k < x_count else None

        along = [central(*(near(c, k) for k in (-2, -1, 1, 2))) for c in range(comps)]
        layers = [layer_derivative(u(c, x)) for c in range(comps)]
        grads = gradients(along, [across[c][x] for c in range(comps)], layers, metric)
        s11, s22, s33, s12, s13, s23 = all_stresses(grads, metric[3], metric[4])
        s_x[0, x], s_x[1, x], s_x[2, x] = s11, s12, s13
        s_o[0, x], s_o[1, x], s_o[2, x] = s22, s23, s33

    metric = [
        edge_tile(
            first_edge[comps + m], first_edge_in[0][comps + m], first_edge_in[-1][comps + m],
            has_left, has_right, window,
        )
        for m in range(5)
    ]
    along, beside = [], []
    for edge in edges:

        def near(k):
            inside = (place + k < x_count) if k > 0 else (place + k >= 0)
            return jnp.where(inside, roll(edge, -window * k), 0.0)

        along.append(central(*(near(k) for k in (-2, -1, 1, 2))))
        beside.append(central(*(roll(edge, -k) for k in (-2, -1, 1, 2))))
    grads = gradients(along, beside, [layer_derivative(edge) for edge in edges], metric)
    _, e22, _, e12, _, e23 = all_stresses(grads, metric[3], metric[4])
    e_s[0], e_s[1], e_s[2], e_s[3], e_s[4] = e12, e22, e23, metric[3], metric[4]


def wide_kernel(
    far, fixed, send, far_ref, near_ref, halo_ref, before_ref, metric_ref, push_ref, first_halo, s_x,
    s_o, e_s, *refs,
):
    out_ref, out_edge, *sends = refs[-3:] if send else refs[-2:]
    terms = refs[0] if fixed else None
    x_count, rows, y_count = metric_ref.shape[1:]
    half, window = x_count // 2, y_count // x_count
    comps = s_x.shape[0]
    side = Side(far, x_count)
    inner = halves(far_ref, near_ref, half)
    band = band_matrix(y_count)
    steps = (-2, -1, 1, 2)

    def u(c, x):
        return inner(c, x) if 0 <= x < x_count else side.halo(halo_ref, c, x, terms)

    def beyond(x):
        return x < 0 if far else x >= x_count

    along_x, others = {}, {}
    for x in range(side.inside[0] - 2, side.inside[-1] + 3):
        if beyond(x):
            continue
        values = [s_x[i, x] for i in range(3)]
        rest = [s_o[i, x] for i in range(3)] if x in side.inside else None
        if any(beyond(x + k) for k in steps):
            add = [
                central(*(u(c, x + k) if beyond(x + k) else None for k in steps))
                for c in range(comps)
            ]
            lame, shear = metric_ref[3, x], metric_ref[4, x]
            pressure = lame * add[0]
            values[0] = values[0] + pressure + (shear + shear) * add[0]
            values[1] = values[1] + shear * add[1]
            values[2] = values[2] + shear * add[2]
            rest[0] = rest[0] + pressure
            rest[2] = rest[2] + pressure
        along_x[x], others[x] = values, rest

    across = [
        banded(jnp.concatenate([u(c, x) for x in side.outside], 0), band) for c in range(2)
    ]
    for place, x in enumerate(side.outside):
        lame, shear = (side.modulus(first_halo, m, x) for m in range(2))
        dx = [
            central(*(u(c, x + k) if 0 <= x + k < x_count else None for k in steps))
            for c in range(comps)
        ]
        dy = [across[c][place * rows : (place + 1) * rows] for c in range(2)]
        values = [side.own_part(halo_ref, i, x, terms) for i in range(3)]
        values[0] = values[0] + lame * (dx[0] + dy[1]) + (shear + shear) * dx[0]
        values[1] = values[1] + shear * (dy[0] + dx[1])
        values[2] = values[2] + shear * dx[2]
        along_x[x] = values

    def across_of(i, x):
        return along_x[x][1] if i == 0 else others[x][i - 1]

    beside = []
    for i in range(comps):
        result = banded(jnp.concatenate([across_of(i, x) for x in side.inside], 0), band)
        added = edge_terms(e_s[i], window)
        beside.append(
            {
                x: result[k * rows : (k + 1) * rows] + edge_spread(added, x, window)
                for k, x in enumerate(side.inside)
            }
        )

    place = lanes_of((rows, y_count)) // window
    messages = [None] * comps
    for k, x in enumerate(side.inside):
        slope_x, slope_y, stretch = (metric_ref[m, x] for m in range(3))
        r11, r12, r13 = (layer_derivative(value) for value in along_x[x])
        r22, r23, r33 = (layer_derivative(value) for value in others[x])
        layers = ((r11, r12, r13), (r12, r22, r23), (r13, r23, r33))
        for c in range(comps):
            force = central(*(along_x[x + j][c] for j in steps)) + beside[c][x]
            force = force + slope_x * layers[c][0] + slope_y * layers[c][1]
            force = force + stretch * layers[c][2]
            at = c * half + k
            following = 2.0 * inner(c, x) - before_ref[at] + force * push_ref[x]
            out_ref[at] = following
            moved = roll(following, window * x + 4)
            messages[c] = moved if k == 0 else jnp.where(place == x, moved, messages[c])
    for c in range(comps):
        out_edge[c] = messages[c]
    if send:
        side.send(
            sends[0],
            lambda c, x: out_ref[c * half + x - side.inside[0]],
            lambda m, x: metric_ref[m, x],
        )


def fix_kernel(sides, *refs):
    corner_in = refs[:sides]
    first_far, first_near, e_s, push_ref = refs[sides : 4 + sides]
    in_far, in_near, far_edge, near_edge = refs[4 + sides : 8 + sides]
    out_far, out_near, *out_edge = refs[8 + sides :]
    x_count, rows, y_count = push_ref.shape
    half, window = x_count // 2, y_count // x_count
    comps = far_edge.shape[0]
    has_left, has_right = neighbours()
    place = lanes_of((rows, y_count)) // window
    lame, shear = 3, 4
    steps = (-2, -1, 1, 2)

    corners = [corner_tile(corner_in, c, window, has_left, has_right) for c in range(2)]
    terms = [edge_terms(corner, window) for corner in corners]
    beside = [
        edge_terms(e_s[shear] * beyond_change(corners[1], window, x_count), window),
        edge_terms(e_s[lame] * beyond_change(corners[0], window, x_count), window),
    ]
    for c in range(comps):
        message = jnp.where(place < half, far_edge[c], near_edge[c])
        for far, first, in_ref, out_ref in (
            (True, first_far, in_far, out_far),
            (False, first_near, in_near, out_near),
        ):
            side = Side(far, x_count)
            changes = {}
            if c < 2:
                changes = {
                    x: side.modulus(first, c, x)
                    * edge_spread(terms[1 - c], x % x_count, window)
                    for x in side.outside
                }
            for k, x in enumerate(side.inside):
                value = in_ref[c * half + k]
                near = [changes.get(x + j) for j in steps]
                if any(item is not None for item in near):
                    change = central(*near) + edge_spread(beside[c], x, window)
                    value = value + change * push_ref[x]
                    message = jnp.where(place == x, roll(value, window * x + 4), message)
                out_ref[c * half + k] = value
        if out_edge:
            out_edge[0][c] = message


def partner_kernel(sides, edge_ref, *refs):
    edge_in = refs[:sides]
    metric_ref, first_far, first_near = refs[sides : 3 + sides]
    moduli_in = refs[3 + sides : 3 + 2 * sides]
    out_ref = refs[3 + 2 * sides]
    x_count, _, y_count = metric_ref.shape[1:]
    window = y_count // x_count
    has_left, has_right = neighbours()
    edges = [
        edge_tile(edge_ref[c], edge_in[0][c], edge_in[-1][c], has_left, has_right, window)
        for c in range(2)
    ]
    lame, shear = (corner_tile(moduli_in, 2 + m, window, has_left, has_right) for m in range(2))
    terms = [edge_terms(edge, window) for edge in edges]
    beside = [
        edge_terms(shear * beyond_change(edges[1], window, x_count), window),
        edge_terms(lame * beyond_change(edges[0], window, x_count), window),
    ]
    for far, first in ((True, first_far), (False, first_near)):
        side = Side(far, x_count)
        added = {}
        for c in range(2):
            changes = {
                x: metric_ref[3 + c, x] * edge_spread(terms[1 - c], x, window)
                for x in (side.inside[:2] if far else side.inside[-2:])
            }
            for x in side.outside:
                near = [changes.get(x + k) for k in (-2, -1, 1, 2)]
                change = central(*near) + edge_spread(beside[c], x % x_count, window)
                change = change * side.packed(first, 0, x, window)
                added[c, x] = out_ref[side.slot(c, x)] = change
        for x in side.outside:
            slope_x, slope_y, stretch = (side.packed(first, 1 + m, x, window) for m in range(3))
            own_lame, own_shear = (side.modulus(first, m, x) for m in range(2))
            dr = [layer_derivative(added[c, x]) for c in range(2)]
            near = [added.get((c, x + k)) for c in range(2) for k in (-2, -1, 1, 2)]
            dx = [central(*near[:4]), central(*near[4:])]
            g11 = dx[0] + slope_x * dr[0]
            out_ref[side.slot(2, x)] = (
                own_lame * (g11 + slope_y * dr[1]) + (own_shear + own_shear) * g11
            )
            out_ref[side.slot(3, x)] = own_shear * (slope_y * dr[0] + dx[1] + slope_x * dr[1])
            out_ref[side.slot(4, x)] = own_shear * (stretch * dr[0])


def sketch_kernel(moment, last, shape, *refs):
    comps, half, rows, y_count = shape
    far_ref, near_ref, before_far, before_near, probe_ref = refs[:5]
    sketch_in = None if moment == 0 else refs[5]
    sketch_ref, spread = refs[-2:]
    x_count = 2 * half
    groups = rows // SUB
    picked = groups // 2
    now = halves(far_ref, near_ref, half)
    past = halves(before_far, before_near, half)
    odd = is_odd()
    spread[...] = jnp.zeros_like(spread)
    spread[pl.ds(0, y_count // 2, stride=2), :] = probe_ref[moment]
    rates = []
    for x in range(0, x_count, 2):
        for c in range(comps):
            rate = now(c, x) - past(c, x)
            other = now(c, x_count - 1 - x) - past(c, x_count - 1 - x)
            rate = jnp.where(odd, -other if c == 0 else other, rate) * (0.5 / time_step)
            rates += [rate[SUB * v : SUB * (v + 1)] for v in range(0, groups, 2)]
    sketch = jnp.dot(
        jnp.concatenate(rates, 0),
        spread[...],
        precision=lax.Precision.HIGHEST,
        preferred_element_type=jnp.float32,
    )
    if sketch_in is not None:
        sketch = sketch + sketch_in[...]
    if last:
        for k in range(half * comps):
            for v in range(picked):
                start = (k * picked + v) * SUB
                sketch_ref[pl.ds(k * picked * SUB + v, SUB, stride=picked), :] = sketch[
                    start : start + SUB
                ]
    else:
        sketch_ref[...] = sketch


def finish_kernel(half, rows, far_ref, near_ref, out_ref):
    x_count, groups = 2 * half, rows // SUB
    now = halves(far_ref, near_ref, half)
    odd = is_odd()
    for c in range(out_ref.shape[0]):
        values = mirrored([now(c, x) for x in range(x_count)], odd, c == 0)
        for x, value in enumerate(values):
            for v in range(groups):
                out_ref[c, pl.ds(x_count * v + x, SUB, stride=groups * x_count), :] = value[
                    SUB * v : SUB * (v + 1)
                ]


def gram_kernel(*refs):
    sum_ref, packed_ref = refs[-2:]
    total = sum_of([ref[...] for ref in refs[:-2]])
    sum_ref[...] = total
    gram = lax.dot_general(
        total,
        total,
        (((0,), (0,)), ((), ())),
        precision=lax.Precision.HIGHEST,
        preferred_element_type=jnp.float32,
    )
    order = gram.shape[0]
    mid = order // 2
    top, bottom = gram[:mid], gram[mid:]
    row = lax.broadcasted_iota(jnp.int32, (mid, order), 0)
    column = lanes_of((mid, order)) - mid
    packed_ref[:mid] = jnp.where((column >= 0) & (row >= column), roll(top, mid), bottom)
    diagonal = jnp.sum(jnp.where(row == column, bottom, 0.0), 0, keepdims=True)
    packed_ref[mid:] = jnp.broadcast_to(diagonal, (packed_ref.shape[0] - mid, order))


def unpacked(packed):
    order = packed.shape[1]
    mid = order // 2
    row = lax.broadcasted_iota(jnp.int32, (mid, order), 0)
    lane = lanes_of((mid, order))
    column = lane - mid
    main = packed[:mid]
    diagonal = jnp.broadcast_to(packed[mid : mid + 1], (mid, order))
    moved = roll(main, mid)
    top = jnp.where(row > lane, moved, jnp.where(row == lane, 0.5 * moved, 0.0))
    bottom = jnp.where(
        (column < 0) | (row < column), main, jnp.where(row == column, 0.5 * diagonal, 0.0)
    )
    part = jnp.concatenate([top, bottom], 0)
    return part + part.T


def factor_kernel(scale, tall_ref, *refs):
    basis_ref, factor_ref = refs[-2:]
    gram = unpacked(sum_of([ref[...] for ref in refs[:-2]]))
    order = gram.shape[0]
    blocks = order // SUB
    shape = (SUB, order)
    sub = lax.broadcasted_iota(jnp.int32, shape, 0)
    lane = lanes_of(shape)
    work = [gram[SUB * q : SUB * (q + 1)] for q in range(blocks)]
    other = [jnp.where(lane == sub + SUB * q, 1.0, 0.0) for q in range(blocks)]
    inverse_rows = []

    def row_of(value, k):
        return jnp.broadcast_to(value[k : k + 1, :], value.shape)

    def column_of(value, j):
        return jnp.broadcast_to(value[:, j : j + 1], value.shape)

    for p in range(blocks):
        columns = [column_of(work[p], SUB * p + k) for k in range(SUB)]
        after_panel = min(p + 1 + AHEAD, blocks)
        ahead = {
            q: [column_of(work[q], SUB * p + k) for k in range(SUB)]
            for q in range(p + 1, after_panel)
        }
        upper = solved = work[p]
        lower = solved_other = other[p]
        pivots = inverses = columns[0]
        for k in range(SUB):
            pivot = row_of(columns[k], k)
            inverse = 1.0 / pivot
            every = jnp.where(sub != k, columns[k] * inverse, 0.0)
            after = jnp.where(sub > k, every, 0.0)
            for m in range(k + 1, SUB):
                columns[m] = columns[m] - every * row_of(columns[m], k)
            upper = upper - after * row_of(upper, k)
            lower = lower - after * row_of(lower, k)
            solved = solved - every * row_of(solved, k)
            solved_other = solved_other - every * row_of(solved_other, k)
            pivots = jnp.where(sub == k, pivot, pivots)
            inverses = jnp.where(sub == k, inverse, inverses)
        root = lax.rsqrt(pivots)
        factor_ref[SUB * p : SUB * (p + 1), :] = jnp.where(lane >= sub + SUB * p, upper * root, 0.0)
        inverse_rows.append(lower * root * scale)
        solved, solved_other = solved * inverses, solved_other * inverses
        for q, entries in ahead.items():
            for k, column in enumerate(entries):
                work[q] = work[q] - column * row_of(solved, k)
                other[q] = other[q] - column * row_of(solved_other, k)
        if after_panel < blocks:
            both = jnp.concatenate([solved, solved_other], 1)
            parts = [jnp.zeros((SUB * p, 2 * order), jnp.float32)] if p else []
            parts += [both, jnp.zeros((order - SUB * (p + 1), 2 * order), jnp.float32)]
            change = jnp.dot(
                jnp.concatenate(work[after_panel:], 0),
                jnp.concatenate(parts, 0),
                precision=lax.Precision.HIGHEST,
                preferred_element_type=jnp.float32,
            )
            for i, q in enumerate(range(after_panel, blocks)):
                work[q] = work[q] - change[SUB * i : SUB * (i + 1), :order]
                other[q] = other[q] - change[SUB * i : SUB * (i + 1), order:]

    inverse_lower = jnp.concatenate(inverse_rows, 0)
    count, kept = basis_ref.shape[0], basis_ref.shape[1]
    start = pl.multiple_of(lax.axis_index("gy") * kept, SUB)
    tall = jnp.concatenate([tall_ref[k, pl.ds(start, kept), :] for k in range(count)], 0)
    basis = lax.dot_general(
        tall,
        inverse_lower,
        (((1,), (1,)), ((), ())),
        precision=lax.Precision.HIGHEST,
        preferred_element_type=jnp.float32,
    )
    for k in range(count):
        basis_ref[k] = basis[k * kept : (k + 1) * kept]


def f32(*shape):
    return jax.ShapeDtypeStruct(shape, jnp.float32)


VMEM = pl.BlockSpec(memory_space=pltpu.MemorySpace.VMEM)
ANY = pl.BlockSpec(memory_space=pl.ANY)
HBM = pl.BlockSpec(memory_space=pltpu.MemorySpace.HBM)


def call(kernel, outs, ins, specs=None, scratch=(), flops=0):
    size = sum(math.prod(x.shape) * 4 for x in (*ins, *outs))
    return pl.pallas_call(
        kernel,
        out_shape=outs,
        in_specs=specs or [VMEM] * len(ins),
        out_specs=[VMEM] * len(outs),
        scratch_shapes=list(scratch),
        compiler_params=pltpu.CompilerParams(vmem_limit_bytes=24 * 2**20),
        cost_estimate=pl.CostEstimate(flops=flops, bytes_accessed=size, transcendentals=0),
    )(*ins)


def butterfly(value, axis):
    count = lax.axis_size(axis)
    if count & (count - 1):
        return [lax.psum(value, axis)]
    bit, terms = 1, [value]
    while bit < count:
        value = sum_of(terms)
        moves = [bit] if 2 * bit == count else [bit, 2 * bit, 3 * bit]
        others = [
            lax.ppermute(value, axis, [(i, i ^ move) for i in range(count)]) for move in moves
        ]
        terms = [value, *others]
        bit *= 2 if len(moves) == 1 else 4
    return terms


def sum_of(terms):
    if len(terms) == 1:
        return terms[0]
    return sum_of(terms[: len(terms) // 2]) + sum_of(terms[len(terms) // 2 :])


def shards(displacement, velocity, slopes, stretch, moduli, buoyancy, probes):
    comps, layers, x_count, y_count = displacement.shape
    width = probes.shape[2]
    half = x_count // 2
    n_x, n_y = lax.axis_size("gx"), lax.axis_size("gy")
    sides = 1 if n_y == 2 else 2

    def flat(array):
        return array.reshape(array.shape[:-3] + (layers * x_count, y_count))

    def exchange(value, far):
        pairs = [(i, i + 1) for i in range(1 if far else 0, n_x - 1, 2)]
        return lax.ppermute(value, "gx", pairs + [(k, i) for i, k in pairs])

    def along_y(value):
        if sides == 1:
            return [lax.ppermute(value, "gy", [(0, 1), (1, 0)])]
        return [
            lax.ppermute(value, "gy", [(i, i + s) for i in range(n_y) if 0 <= i + s < n_y])
            for s in (1, -1)
        ]

    def slabs(count):
        return f32(count, layers, y_count)

    u_flat = flat(displacement)
    fields = [
        pltpu.with_memory_space_constraint(field, pltpu.MemorySpace.HBM)
        for field in (u_flat, flat(slopes), flat(stretch), flat(moduli), flat(buoyancy))
    ]
    u_far, u_near, far_send, near_send, edge, metric = call(
        begin_kernel,
        [
            slabs(comps * half), slabs(comps * half), slabs(17), slabs(17), slabs(comps + 5),
            f32(5, x_count, layers, y_count),
        ],
        fields,
        specs=[HBM] * 5,
        scratch=[pltpu.VMEM(field.shape, jnp.float32) for field in fields]
        + [pltpu.SemaphoreType.DMA((5,))],
    )
    before_far, before_near, push = call(
        rest_kernel,
        [slabs(comps * half), slabs(comps * half), slabs(x_count)],
        [u_flat, flat(velocity), flat(buoyancy)],
    )

    sketch_rows = half * comps * (layers // 2)
    sketch = []

    def half_step(far, moment, halo, first_halo, before, terms, token):
        return call(
            partial(wide_kernel, far, len(terms), moment < STEPS - 1),
            [slabs(comps * half), slabs(comps)] + ([slabs(12)] if moment < STEPS - 1 else []),
            [
                u_far, u_near, halo, before, metric, push, first_halo, s_x, s_o, e_s, *terms, *token,
            ],
            specs=[VMEM] * (10 + len(terms)) + [ANY] * len(token),
            flops=10_000_000,
        )

    terms = []
    for moment in range(STEPS):
        last = moment == STEPS - 1
        if moment == 0:
            far_halo = exchange(far_send, True)
            near_halo = exchange(near_send, False)
        edge_in = along_y(edge)
        if moment == 0:
            first_edge, first_edge_in, first_far, first_near = edge, edge_in, far_halo, near_halo
        s_x, s_o, e_s = call(
            partial(tile_kernel, sides, comps),
            [f32(comps, x_count, layers, y_count), f32(3, x_count, layers, y_count), slabs(5)],
            [u_far, u_near, edge, *edge_in, metric, first_edge, *first_edge_in],
            flops=20_000_000,
        )
        raw_far, far_edge, *far_send = half_step(
            True, moment, far_halo, first_far, before_far, terms, sketch or [push, near_halo]
        )
        (corner,) = call(
            partial(corner_kernel, x_count, len(terms)),
            [slabs(2 if moment else 4)],
            [far_halo, near_halo, *terms, raw_far],
            specs=[VMEM] * (2 + len(terms)) + [ANY],
        )
        corner_in = along_y(corner)
        if moment == 0:
            moduli_in = corner_in
        raw_near, near_edge, *near_send = half_step(
            False, moment, near_halo, first_near, before_near, terms, [raw_far]
        )
        if not last:
            far_halo = exchange(far_send[0], True)
            near_halo = exchange(near_send[0], False)
            terms = call(
                partial(partner_kernel, sides),
                [slabs(20)],
                [edge, *edge_in, metric, first_far, first_near, *moduli_in],
            )
        next_far, next_near, *edge = call(
            partial(fix_kernel, sides),
            [slabs(comps * half), slabs(comps * half)] + ([] if last else [slabs(comps)]),
            [
                *corner_in, first_far, first_near, e_s, push, raw_far, raw_near, far_edge, near_edge,
            ],
        )
        edge = None if last else edge[0]
        sketch = call(
            partial(sketch_kernel, moment, last, (comps, half, layers, y_count)),
            [f32(sketch_rows, width)],
            [next_far, next_near, before_far, before_near, probes, *sketch],
            scratch=[pltpu.VMEM((y_count, width), jnp.float32)],
        )
        before_far, before_near, u_far, u_near = u_far, u_near, next_far, next_near
    (final,) = call(
        partial(finish_kernel, half, layers),
        [f32(comps, layers * x_count, y_count)],
        [u_far, u_near],
    )
    final = final.reshape(displacement.shape)

    parts = butterfly(sketch[0], "gy")
    tall, packed = call(gram_kernel, [f32(sketch_rows, width), f32(width // 2 + SUB, width)], parts)
    parts = butterfly(packed, "gx")
    depth = comps * (layers // 2)
    basis, factor = call(
        partial(factor_kernel, math.sqrt(sketch_rows * n_x)),
        [f32(half, depth // n_y, width), f32(width, width)],
        [tall.reshape(half, depth, width), *parts],
    )
    return (final, basis, factor)


def solution(mesh):
    in_specs = (
        P(None, None, "gx", "gy"),
        P(None, None, "gx", "gy"),
        P(None, None, "gx", "gy"),
        P(None, "gx", "gy"),
        P(None, None, "gx", "gy"),
        P(None, "gx", "gy"),
        P(None, "gy", None),
    )
    out_specs = (P(None, None, "gx", "gy"), P("gx", "gy", None), P())

    return jax.shard_map(shards, mesh=mesh, in_specs=in_specs, out_specs=out_specs, check_vma=False)
```

profile of v0, /device:TPU:0, one launch (start us, length us, event | category | flops | bytes accessed | tf_op | source)
XLA Modules:
  0.0 78.0 jit_solution(2009075613625325648)
XLA Ops:
  0.7 2.2 %shard_map.94 = (f32[12,32,128]{2,1,0:T(8,128)S(1)}, f32[12,32,128]{2,1,0:T(8,128)S(1)}, f32[17,32,128]{2,1,0:T(8,128)S(1)}, f32[17,32,128]{2,1,0:T(8,128)S(1)},...) custom-call(f32[3,256,128]{2,1,0:T(8,128)} %bitcast.8, f32[2,256,128]{2,1,0:T(8,128)} %bitcast.15, ...), custom_call_target="tpu_custom_call" | custom-call | bytes 2916352 | tf_op jit(solution)/shard_map/pallas_call | solution.py:755
  2.8 3.0 %collective-permute-start.2 = (f32[17,32,128]{2,1,0:T(8,128)S(1)}, f32[17,32,128]{2,1,0:T(8,128)S(1)}, u32[]{:S(2)}, u32[]{:S(2)}) collective-permute-start(f32[17,32,128]{2,1,0:T(8,128)S(1)} %get-tuple-element.71), channel_id=1, source_target_pairs={{0,2},{4,6},{8,10},{12,14},{16,18},{20,22},{24,26},{28,30},{2,0},{... | collective-permute-start | bytes 835592 | tf_op jit(solution)/shard_map/ppermute | solution.py:800
  8.5 9.2 %collective-permute-done.2.refs_1_.halo_ref.first_halo.near_ref.refs_3_.refs_2_ = f32[17,32,128]{2,1,0:T(8,128)S(1)} collective-permute-done((f32[17,32,128]{2,1,0:T(8,128)S(1)}, f32[17,32,128]{2,1,0:T(8,128)S(1)}, u32[]{:S(2)}, u32[]{:S(2)}) %collective-permute-start.2) | collective-permute-done | bytes 278560 | tf_op jit(solution)/shard_map/ppermute | solution.py:800
  19.3 5.0 %collective-permute-start.4 = (f32[12,32,128]{2,1,0:T(8,128)S(1)}, f32[12,32,128]{2,1,0:T(8,128)S(1)}, u32[]{:S(2)}, u32[]{:S(2)}) collective-permute-start(f32[12,32,128]{2,1,0:T(8,128)S(1)} %get-tuple-element.75), channel_id=1, source_target_pairs={{0,2},{4,6},{8,10},{12,14},{16,18},{20,22},{24,26},{28,30},{2,0},{... | collective-permute-start | bytes 589832 | tf_op jit(solution)/shard_map/ppermute | solution.py:800
  24.5 1.2 %collective-permute-done.5.refs_4_.refs_0_ = f32[4,32,128]{2,1,0:T(8,128)S(1)} collective-permute-done((f32[4,32,128]{2,1,0:T(8,128)S(1)}, f32[4,32,128]{2,1,0:T(8,128)S(1)}, u32[]{:S(2)}, u32[]{:S(2)}) %collective-permute-start.5) | collective-permute-done | bytes 65568 | tf_op jit(solution)/shard_map/ppermute | solution.py:804
  29.2 2.8 %collective-permute-done.4.near_ref.halo_ref = f32[12,32,128]{2,1,0:T(8,128)S(1)} collective-permute-done((f32[12,32,128]{2,1,0:T(8,128)S(1)}, f32[12,32,128]{2,1,0:T(8,128)S(1)}, u32[]{:S(2)}, u32[]{:S(2)}) %collective-permute-start.4) | collective-permute-done | bytes 196640 | tf_op jit(solution)/shard_map/ppermute | solution.py:800
  32.5 2.9 %collective-permute-start.11 = (f32[12,32,128]{2,1,0:T(8,128)S(1)}, f32[12,32,128]{2,1,0:T(8,128)S(1)}, u32[]{:S(2)}, u32[]{:S(2)}) collective-permute-start(f32[12,32,128]{2,1,0:T(8,128)S(1)} %get-tuple-element.97), channel_id=1, source_target_pairs={{0,2},{4,6},{8,10},{12,14},{16,18},{20,22},{24,26},{28,30},{2,0},{... | collective-permute-start | bytes 589832 | tf_op jit(solution)/shard_map/ppermute | solution.py:800
  35.5 1.2 %collective-permute-done.7.refs_0_ = f32[2,32,128]{2,1,0:T(8,128)S(1)} collective-permute-done((f32[2,32,128]{2,1,0:T(8,128)S(1)}, f32[2,32,128]{2,1,0:T(8,128)S(1)}, u32[]{:S(2)}, u32[]{:S(2)}) %collective-permute-start.7) | collective-permute-done | bytes 32800 | tf_op jit(solution)/shard_map/ppermute | solution.py:804
  39.5 0.9 %collective-permute-start.10 = (f32[12,32,128]{2,1,0:T(8,128)S(1)}, f32[12,32,128]{2,1,0:T(8,128)S(1)}, u32[]{:S(2)}, u32[]{:S(2)}) collective-permute-start(f32[12,32,128]{2,1,0:T(8,128)S(1)} %get-tuple-element.96), channel_id=1, source_target_pairs={{2,4},{6,8},{10,12},{14,16},{18,20},{22,24},{26,28},{4,2},{8,6},{1... | collective-permute-start | bytes 589832 | tf_op jit(solution)/shard_map/ppermute | solution.py:800
  40.4 1.9 %collective-permute-done.11.halo_ref.near_ref = f32[12,32,128]{2,1,0:T(8,128)S(1)} collective-permute-done((f32[12,32,128]{2,1,0:T(8,128)S(1)}, f32[12,32,128]{2,1,0:T(8,128)S(1)}, u32[]{:S(2)}, u32[]{:S(2)}) %collective-permute-start.11) | collective-permute-done | bytes 196640 | tf_op jit(solution)/shard_map/ppermute | solution.py:800
  42.8 3.5 %collective-permute-start.12 = (f32[12,32,128]{2,1,0:T(8,128)S(1)}, f32[12,32,128]{2,1,0:T(8,128)S(1)}, u32[]{:S(2)}, u32[]{:S(2)}) collective-permute-start(f32[12,32,128]{2,1,0:T(8,128)S(1)} %get-tuple-element.99), channel_id=1, source_target_pairs={{0,2},{4,6},{8,10},{12,14},{16,18},{20,22},{24,26},{28,30},{2,0},{... | collective-permute-start | bytes 589832 | tf_op jit(solution)/shard_map/ppermute | solution.py:800
  46.4 1.2 %collective-permute-done.13.refs_0_ = f32[2,32,128]{2,1,0:T(8,128)S(1)} collective-permute-done((f32[2,32,128]{2,1,0:T(8,128)S(1)}, f32[2,32,128]{2,1,0:T(8,128)S(1)}, u32[]{:S(2)}, u32[]{:S(2)}) %collective-permute-start.13) | collective-permute-done | bytes 32800 | tf_op jit(solution)/shard_map/ppermute | solution.py:804
  50.4 2.9 %collective-permute-done.12.near_ref.halo_ref = f32[12,32,128]{2,1,0:T(8,128)S(1)} collective-permute-done((f32[12,32,128]{2,1,0:T(8,128)S(1)}, f32[12,32,128]{2,1,0:T(8,128)S(1)}, u32[]{:S(2)}, u32[]{:S(2)}) %collective-permute-start.12) | collective-permute-done | bytes 196640 | tf_op jit(solution)/shard_map/ppermute | solution.py:800
  55.5 1.1 %collective-permute-done.16.refs_1_ = f32[192,128]{1,0:T(8,128)S(1)} collective-permute-done((f32[192,128]{1,0:T(8,128)S(1)}, f32[192,128]{1,0:T(8,128)S(1)}, u32[]{:S(2)}, u32[]{:S(2)}) %collective-permute-start.16) | collective-permute-done | bytes 98336 | tf_op jit(solution)/shard_map/ppermute | solution.py:775
  57.1 2.5 %collective-permute-start.17 = (f32[72,128]{1,0:T(8,128)S(1)}, f32[72,128]{1,0:T(8,128)S(1)}, u32[]{:S(2)}, u32[]{:S(2)}) collective-permute-start(f32[72,128]{1,0:T(8,128)S(1)} %get-tuple-element.116), channel_id=1, source_target_pairs={{0,2},{2,0},{4,6},{6,4},{8,10},{10,8},{12,14},{14,12},{16,18},{18,... | collective-permute-start | bytes 110600 | tf_op jit(solution)/shard_map/ppermute | solution.py:775
  59.6 1.5 %collective-permute-start.19 = (f32[72,128]{1,0:T(8,128)S(1)}, f32[72,128]{1,0:T(8,128)S(1)}, u32[]{:S(2)}, u32[]{:S(2)}) collective-permute-start(f32[72,128]{1,0:T(8,128)S(1)} %get-tuple-element.116), channel_id=1, source_target_pairs={{0,6},{2,4},{4,2},{6,0},{8,14},{10,12},{12,10},{14,8},{16,22},{18,... | collective-permute-start | bytes 110600 | tf_op jit(solution)/shard_map/ppermute | solution.py:775
  61.5 2.2 %collective-permute-done.18 = f32[72,128]{1,0:T(8,128)S(1)} collective-permute-done((f32[72,128]{1,0:T(8,128)S(1)}, f32[72,128]{1,0:T(8,128)S(1)}, u32[]{:S(2)}, u32[]{:S(2)}) %collective-permute-start.18) | collective-permute-done | bytes 36896 | tf_op jit(solution)/shard_map/ppermute | solution.py:775
  64.5 1.8 %collective-permute-start.20 = (f32[72,128]{1,0:T(8,128)S(1)}, f32[72,128]{1,0:T(8,128)S(1)}, u32[]{:S(2)}, u32[]{:S(2)}) collective-permute-start(f32[72,128]{1,0:T(8,128)S(1)} %add_add_fusion.refs_0_), channel_id=1, source_target_pairs={{0,8},{2,10},{4,12},{6,14},{8,0},{10,2},{12,4},{14,6},{16,24},{18,... | collective-permute-start | bytes 110600 | tf_op jit(solution)/shard_map/ppermute | solution.py:775
  66.3 1.6 %collective-permute-start.21 = (f32[72,128]{1,0:T(8,128)S(1)}, f32[72,128]{1,0:T(8,128)S(1)}, u32[]{:S(2)}, u32[]{:S(2)}) collective-permute-start(f32[72,128]{1,0:T(8,128)S(1)} %add_add_fusion.refs_0_), channel_id=1, source_target_pairs={{0,16},{2,18},{4,20},{6,22},{8,24},{10,26},{12,28},{14,30},{16,0},... | collective-permute-start | bytes 110600 | tf_op jit(solution)/shard_map/ppermute | solution.py:775
  67.8 1.1 %collective-permute-start.22 = (f32[72,128]{1,0:T(8,128)S(1)}, f32[72,128]{1,0:T(8,128)S(1)}, u32[]{:S(2)}, u32[]{:S(2)}) collective-permute-start(f32[72,128]{1,0:T(8,128)S(1)} %add_add_fusion.refs_0_), channel_id=1, source_target_pairs={{0,24},{2,26},{4,28},{6,30},{8,16},{10,18},{12,20},{14,22},{16,8},... | collective-permute-start | bytes 110600 | tf_op jit(solution)/shard_map/ppermute | solution.py:775
  68.9 1.0 %shard_map.122 = f32[3,256,128]{2,1,0:T(8,128)} custom-call(f32[12,32,128]{2,1,0:T(8,128)S(1)} %get-tuple-element.113.far_ref.refs_0_, f32[12,32,128]{2,1,0:T(8,128)S(1)} %get-tuple-element.114.near_ref.refs_1_), custom_call_target="tpu_custom_call" | custom-call | bytes 786432 | tf_op jit(solution)/shard_map/pallas_call | solution.py:755
  69.9 1.9 %collective-permute-done.21.refs_2_ = f32[72,128]{1,0:T(8,128)S(1)} collective-permute-done((f32[72,128]{1,0:T(8,128)S(1)}, f32[72,128]{1,0:T(8,128)S(1)}, u32[]{:S(2)}, u32[]{:S(2)}) %collective-permute-start.21) | collective-permute-done | bytes 36896 | tf_op jit(solution)/shard_map/ppermute | solution.py:775
  71.8 1.8 %collective-permute-done.22.refs_3_ = f32[72,128]{1,0:T(8,128)S(1)} collective-permute-done((f32[72,128]{1,0:T(8,128)S(1)}, f32[72,128]{1,0:T(8,128)S(1)}, u32[]{:S(2)}, u32[]{:S(2)}) %collective-permute-start.22) | collective-permute-done | bytes 36896 | tf_op jit(solution)/shard_map/ppermute | solution.py:775
  73.6 4.4 %shard_map.125 = (f32[4,24,128]{2,1,0:T(8,128)}, f32[128,128]{1,0:T(8,128)}) custom-call(f32[4,48,128]{2,1,0:T(8,128)S(1)} %bitcast.13, f32[72,128]{1,0:T(8,128)S(1)} %add_add_fusion.refs_0_, f32[72,128]{1,0:T(8,128)S(1)} %collective-permute-done.20.refs_1_, f32[72,128]{1,0:T(8,128)S(1)} %collective-permute-done.21.refs_2_, ...), custom_call_target="tpu_custom_call" | custom-call | bytes 360448 | tf_op jit(solution)/shard_map/pallas_call | solution.py:755
  (63 shorter events, 18.2 us)
Async XLA Ops:
  0.6 6.0 %copy-start.1 = (f32[3,32,8,128]{3,2,1,0:T(8,128)S(1)}, f32[3,32,8,128]{3,2,1,0:T(8,128)}, u32[]{:S(2)}) copy-start(f32[3,32,8,128]{3,2,1,0:T(8,128)} %param.7) | copy-start | bytes 1179652
  2.8 14.9 %collective-permute-start.2 = (f32[17,32,128]{2,1,0:T(8,128)S(1)}, f32[17,32,128]{2,1,0:T(8,128)S(1)}, u32[]{:S(2)}, u32[]{:S(2)}) collective-permute-start(f32[17,32,128]{2,1,0:T(8,128)S(1)} %get-tuple-element.71), channel_id=1, source_target_pairs={{0,2},{4,6},{8,10},{12,14},{16,18},{20,22},{24,26},{28,30},{2,0},{... | collective-permute-start | bytes 835592 | tf_op jit(solution)/shard_map/ppermute | solution.py:800
  5.9 11.9 %collective-permute-start = (f32[17,32,128]{2,1,0:T(8,128)S(1)}, f32[17,32,128]{2,1,0:T(8,128)S(1)}, u32[]{:S(2)}, u32[]{:S(2)}) collective-permute-start(f32[17,32,128]{2,1,0:T(8,128)S(1)} %get-tuple-element.63), channel_id=1, source_target_pairs={{2,4},{6,8},{10,12},{14,16},{18,20},{22,24},{26,28},{4,2},{8,6},{1... | collective-permute-start | bytes 835592 | tf_op jit(solution)/shard_map/ppermute | solution.py:800
  6.5 1.4 %collective-permute-start.1 = (f32[8,32,128]{2,1,0:T(8,128)S(1)}, f32[8,32,128]{2,1,0:T(8,128)S(1)}, u32[]{:S(2)}, u32[]{:S(2)}) collective-permute-start(f32[8,32,128]{2,1,0:T(8,128)S(1)} %get-tuple-element.67.refs_2_.refs_5_.edge_ref), channel_id=1, source_target_pairs={{0,1},{1,0},{2,3},{3,2},{4,5},{5,4},{6,7},{7,6},{8,9},{9,8},{10,11... | collective-permute-start | bytes 393224 | tf_op jit(solution)/shard_map/ppermute | solution.py:804
  18.2 9.9 %collective-permute-start.3 = (f32[12,32,128]{2,1,0:T(8,128)S(1)}, f32[12,32,128]{2,1,0:T(8,128)S(1)}, u32[]{:S(2)}, u32[]{:S(2)}) collective-permute-start(f32[12,32,128]{2,1,0:T(8,128)S(1)} %get-tuple-element.72), channel_id=1, source_target_pairs={{2,4},{6,8},{10,12},{14,16},{18,20},{22,24},{26,28},{4,2},{8,6},{1... | collective-permute-start | bytes 589832 | tf_op jit(solution)/shard_map/ppermute | solution.py:800
  19.3 12.7 %collective-permute-start.4 = (f32[12,32,128]{2,1,0:T(8,128)S(1)}, f32[12,32,128]{2,1,0:T(8,128)S(1)}, u32[]{:S(2)}, u32[]{:S(2)}) collective-permute-start(f32[12,32,128]{2,1,0:T(8,128)S(1)} %get-tuple-element.75), channel_id=1, source_target_pairs={{0,2},{4,6},{8,10},{12,14},{16,18},{20,22},{24,26},{28,30},{2,0},{... | collective-permute-start | bytes 589832 | tf_op jit(solution)/shard_map/ppermute | solution.py:800
  24.4 1.3 %collective-permute-start.5 = (f32[4,32,128]{2,1,0:T(8,128)S(1)}, f32[4,32,128]{2,1,0:T(8,128)S(1)}, u32[]{:S(2)}, u32[]{:S(2)}) collective-permute-start(f32[4,32,128]{2,1,0:T(8,128)S(1)} %shard_map.99), channel_id=1, source_target_pairs={{0,1},{1,0},{2,3},{3,2},{4,5},{5,4},{6,7},{7,6},{8,9},{9,8},{10,11... | collective-permute-start | bytes 196616 | tf_op jit(solution)/shard_map/ppermute | solution.py:804
  26.2 1.3 %collective-permute-start.6 = (f32[3,32,128]{2,1,0:T(8,128)S(1)}, f32[3,32,128]{2,1,0:T(8,128)S(1)}, u32[]{:S(2)}, u32[]{:S(2)}) collective-permute-start(f32[3,32,128]{2,1,0:T(8,128)S(1)} %get-tuple-element.81.refs_2_.edge_ref), channel_id=1, source_target_pairs={{0,1},{1,0},{2,3},{3,2},{4,5},{5,4},{6,7},{7,6},{8,9},{9,8},{10,11... | collective-permute-start | bytes 147464 | tf_op jit(solution)/shard_map/ppermute | solution.py:804
  28.6 10.5 %collective-permute-start.8 = (f32[12,32,128]{2,1,0:T(8,128)S(1)}, f32[12,32,128]{2,1,0:T(8,128)S(1)}, u32[]{:S(2)}, u32[]{:S(2)}) collective-permute-start(f32[12,32,128]{2,1,0:T(8,128)S(1)} %get-tuple-element.91), channel_id=1, source_target_pairs={{2,4},{6,8},{10,12},{14,16},{18,20},{22,24},{26,28},{4,2},{8,6},{1... | collective-permute-start | bytes 589832 | tf_op jit(solution)/shard_map/ppermute | solution.py:800
  32.5 9.8 %collective-permute-start.11 = (f32[12,32,128]{2,1,0:T(8,128)S(1)}, f32[12,32,128]{2,1,0:T(8,128)S(1)}, u32[]{:S(2)}, u32[]{:S(2)}) collective-permute-start(f32[12,32,128]{2,1,0:T(8,128)S(1)} %get-tuple-element.97), channel_id=1, source_target_pairs={{0,2},{4,6},{8,10},{12,14},{16,18},{20,22},{24,26},{28,30},{2,0},{... | collective-permute-start | bytes 589832 | tf_op jit(solution)/shard_map/ppermute | solution.py:800
  35.5 1.3 %collective-permute-start.7 = (f32[2,32,128]{2,1,0:T(8,128)S(1)}, f32[2,32,128]{2,1,0:T(8,128)S(1)}, u32[]{:S(2)}, u32[]{:S(2)}) collective-permute-start(f32[2,32,128]{2,1,0:T(8,128)S(1)} %shard_map.105), channel_id=1, source_target_pairs={{0,1},{1,0},{2,3},{3,2},{4,5},{5,4},{6,7},{7,6},{8,9},{9,8},{10,11... | collective-permute-start | bytes 98312 | tf_op jit(solution)/shard_map/ppermute | solution.py:804
  37.2 1.3 %collective-permute-start.9 = (f32[3,32,128]{2,1,0:T(8,128)S(1)}, f32[3,32,128]{2,1,0:T(8,128)S(1)}, u32[]{:S(2)}, u32[]{:S(2)}) collective-permute-start(f32[3,32,128]{2,1,0:T(8,128)S(1)} %get-tuple-element.92.refs_2_.edge_ref), channel_id=1, source_target_pairs={{0,1},{1,0},{2,3},{3,2},{4,5},{5,4},{6,7},{7,6},{8,9},{9,8},{10,11... | collective-permute-start | bytes 147464 | tf_op jit(solution)/shard_map/ppermute | solution.py:804
  39.5 10.4 %collective-permute-start.10 = (f32[12,32,128]{2,1,0:T(8,128)S(1)}, f32[12,32,128]{2,1,0:T(8,128)S(1)}, u32[]{:S(2)}, u32[]{:S(2)}) collective-permute-start(f32[12,32,128]{2,1,0:T(8,128)S(1)} %get-tuple-element.96), channel_id=1, source_target_pairs={{2,4},{6,8},{10,12},{14,16},{18,20},{22,24},{26,28},{4,2},{8,6},{1... | collective-permute-start | bytes 589832 | tf_op jit(solution)/shard_map/ppermute | solution.py:800
  42.8 10.5 %collective-permute-start.12 = (f32[12,32,128]{2,1,0:T(8,128)S(1)}, f32[12,32,128]{2,1,0:T(8,128)S(1)}, u32[]{:S(2)}, u32[]{:S(2)}) collective-permute-start(f32[12,32,128]{2,1,0:T(8,128)S(1)} %get-tuple-element.99), channel_id=1, source_target_pairs={{0,2},{4,6},{8,10},{12,14},{16,18},{20,22},{24,26},{28,30},{2,0},{... | collective-permute-start | bytes 589832 | tf_op jit(solution)/shard_map/ppermute | solution.py:800
  46.3 1.3 %collective-permute-start.13 = (f32[2,32,128]{2,1,0:T(8,128)S(1)}, f32[2,32,128]{2,1,0:T(8,128)S(1)}, u32[]{:S(2)}, u32[]{:S(2)}) collective-permute-start(f32[2,32,128]{2,1,0:T(8,128)S(1)} %shard_map.114), channel_id=1, source_target_pairs={{0,1},{1,0},{2,3},{3,2},{4,5},{5,4},{6,7},{7,6},{8,9},{9,8},{10,11... | collective-permute-start | bytes 98312 | tf_op jit(solution)/shard_map/ppermute | solution.py:804
  48.1 1.3 %collective-permute-start.14 = (f32[3,32,128]{2,1,0:T(8,128)S(1)}, f32[3,32,128]{2,1,0:T(8,128)S(1)}, u32[]{:S(2)}, u32[]{:S(2)}) collective-permute-start(f32[3,32,128]{2,1,0:T(8,128)S(1)} %get-tuple-element.105.refs_2_), channel_id=1, source_target_pairs={{0,1},{1,0},{2,3},{3,2},{4,5},{5,4},{6,7},{7,6},{8,9},{9,8},{10,11... | collective-permute-start | bytes 147464 | tf_op jit(solution)/shard_map/ppermute | solution.py:804
  53.4 1.3 %collective-permute-start.15 = (f32[2,32,128]{2,1,0:T(8,128)S(1)}, f32[2,32,128]{2,1,0:T(8,128)S(1)}, u32[]{:S(2)}, u32[]{:S(2)}) collective-permute-start(f32[2,32,128]{2,1,0:T(8,128)S(1)} %shard_map.119), channel_id=1, source_target_pairs={{0,1},{1,0},{2,3},{3,2},{4,5},{5,4},{6,7},{7,6},{8,9},{9,8},{10,11... | collective-permute-start | bytes 98312 | tf_op jit(solution)/shard_map/ppermute | solution.py:804
  55.3 1.4 %collective-permute-start.16 = (f32[192,128]{1,0:T(8,128)S(1)}, f32[192,128]{1,0:T(8,128)S(1)}, u32[]{:S(2)}, u32[]{:S(2)}) collective-permute-start(f32[192,128]{1,0:T(8,128)S(1)} %shard_map.123.refs_0_), channel_id=1, source_target_pairs={{0,1},{1,0},{2,3},{3,2},{4,5},{5,4},{6,7},{7,6},{8,9},{9,8},{10,11... | collective-permute-start | bytes 294920 | tf_op jit(solution)/shard_map/ppermute | solution.py:775
  57.1 4.5 %collective-permute-start.17 = (f32[72,128]{1,0:T(8,128)S(1)}, f32[72,128]{1,0:T(8,128)S(1)}, u32[]{:S(2)}, u32[]{:S(2)}) collective-permute-start(f32[72,128]{1,0:T(8,128)S(1)} %get-tuple-element.116), channel_id=1, source_target_pairs={{0,2},{2,0},{4,6},{6,4},{8,10},{10,8},{12,14},{14,12},{16,18},{18,... | collective-permute-start | bytes 110600 | tf_op jit(solution)/shard_map/ppermute | solution.py:775
  59.6 4.2 %collective-permute-start.18 = (f32[72,128]{1,0:T(8,128)S(1)}, f32[72,128]{1,0:T(8,128)S(1)}, u32[]{:S(2)}, u32[]{:S(2)}) collective-permute-start(f32[72,128]{1,0:T(8,128)S(1)} %get-tuple-element.116), channel_id=1, source_target_pairs={{0,4},{2,6},{4,0},{6,2},{8,12},{10,14},{12,8},{14,10},{16,20},{18,... | collective-permute-start | bytes 110600 | tf_op jit(solution)/shard_map/ppermute | solution.py:775
  59.6 4.9 %collective-permute-start.19 = (f32[72,128]{1,0:T(8,128)S(1)}, f32[72,128]{1,0:T(8,128)S(1)}, u32[]{:S(2)}, u32[]{:S(2)}) collective-permute-start(f32[72,128]{1,0:T(8,128)S(1)} %get-tuple-element.116), channel_id=1, source_target_pairs={{0,6},{2,4},{4,2},{6,0},{8,14},{10,12},{12,10},{14,8},{16,22},{18,... | collective-permute-start | bytes 110600 | tf_op jit(solution)/shard_map/ppermute | solution.py:775
  64.5 5.4 %collective-permute-start.20 = (f32[72,128]{1,0:T(8,128)S(1)}, f32[72,128]{1,0:T(8,128)S(1)}, u32[]{:S(2)}, u32[]{:S(2)}) collective-permute-start(f32[72,128]{1,0:T(8,128)S(1)} %add_add_fusion.refs_0_), channel_id=1, source_target_pairs={{0,8},{2,10},{4,12},{6,14},{8,0},{10,2},{12,4},{14,6},{16,24},{18,... | collective-permute-start | bytes 110600 | tf_op jit(solution)/shard_map/ppermute | solution.py:775
  66.3 5.5 %collective-permute-start.21 = (f32[72,128]{1,0:T(8,128)S(1)}, f32[72,128]{1,0:T(8,128)S(1)}, u32[]{:S(2)}, u32[]{:S(2)}) collective-permute-start(f32[72,128]{1,0:T(8,128)S(1)} %add_add_fusion.refs_0_), channel_id=1, source_target_pairs={{0,16},{2,18},{4,20},{6,22},{8,24},{10,26},{12,28},{14,30},{16,0},... | collective-permute-start | bytes 110600 | tf_op jit(solution)/shard_map/ppermute | solution.py:775
  67.8 5.8 %collective-permute-start.22 = (f32[72,128]{1,0:T(8,128)S(1)}, f32[72,128]{1,0:T(8,128)S(1)}, u32[]{:S(2)}, u32[]{:S(2)}) collective-permute-start(f32[72,128]{1,0:T(8,128)S(1)} %add_add_fusion.refs_0_), channel_id=1, source_target_pairs={{0,24},{2,26},{4,28},{6,30},{8,16},{10,18},{12,20},{14,22},{16,8},... | collective-permute-start | bytes 110600 | tf_op jit(solution)/shard_map/ppermute | solution.py:775
  (3 other events, 12.9 us)
where the time goes:
time: 78.2 us; the launch traced here: 78 us
  waiting for transfers between devices  31.1 us (40%)
  starting transfers between devices  27 us (35%)
  Pallas kernels  18.6 us (24%)
  between operations  1 us (1%)
    pallas_call x32, Pallas kernels, call(): pl.pallas_call(kernel, out_shape=outs, in_specs=specs or [VMEM] * len(ins...  18.6 us
    ppermute x8, starting transfers between devices, exchange(): return lax.ppermute(value, 'gx', pairs + [(k, i) for i, k in pairs])  17.2 us
    ppermute x8, waiting for transfers between devices, exchange(): return lax.ppermute(value, 'gx', pairs + [(k, i) for i, k in pairs])  16.9 us
    ppermute x7, starting transfers between devices, butterfly(): lax.ppermute(value, axis, [(i, i ^ move) for i in range(count)])  8.76 us
    ppermute x7, waiting for transfers between devices, butterfly(): lax.ppermute(value, axis, [(i, i ^ move) for i in range(count)])  8.16 us
    ppermute x8, waiting for transfers between devices, along_y(): return [lax.ppermute(value, 'gy', [(0, 1), (1, 0)])]  6.05 us
  transfers between devices with their start and end apart: 23, of which 18 were waited for; matrix products, arithmetic and copies ran while one was open for 0% of the time, Pallas kernels for 14%

commit v1 on v0

--- a/solution.py
+++ b/solution.py
@@ -11,7 +11,7 @@
 
 STEPS = 4
 SUB = 8
-AHEAD = 2
+AHEAD = 3
 
 time_step = 0.12
 
@@ -681,13 +681,16 @@
     def column_of(value, j):
         return jnp.broadcast_to(value[:, j : j + 1], value.shape)
 
+    columns = [column_of(work[0], k) for k in range(SUB)]
     for p in range(blocks):
-        columns = [column_of(work[p], SUB * p + k) for k in range(SUB)]
         after_panel = min(p + 1 + AHEAD, blocks)
         ahead = {
             q: [column_of(work[q], SUB * p + k) for k in range(SUB)]
             for q in range(p + 1, after_panel)
         }
+        more = p + 1 < blocks
+        coming = [column_of(work[p + 1], SUB * (p + 1) + k) for k in range(SUB)] if more else []
+        below = list(ahead[p + 1]) if more else []
         upper = solved = work[p]
         lower = solved_other = other[p]
         pivots = inverses = columns[0]
@@ -697,7 +700,12 @@
             every = jnp.where(sub != k, columns[k] * inverse, 0.0)
             after = jnp.where(sub > k, every, 0.0)
             for m in range(k + 1, SUB):
-                columns[m] = columns[m] - every * row_of(columns[m], k)
+                entry = row_of(columns[m], k)
+                columns[m] = columns[m] - every * entry
+                if more:
+                    below[m] = below[m] - below[k] * (inverse * entry)
+            for j in range(len(coming)):
+                coming[j] = coming[j] - below[k] * inverse * row_of(below[k], j)
             upper = upper - after * row_of(upper, k)
             lower = lower - after * row_of(lower, k)
             solved = solved - every * row_of(solved, k)
@@ -712,6 +720,7 @@
             for k, column in enumerate(entries):
                 work[q] = work[q] - column * row_of(solved, k)
                 other[q] = other[q] - column * row_of(solved_other, k)
+        columns = coming
         if after_panel < blocks:
             both = jnp.concatenate([solved, solved_other], 1)
             parts = [jnp.zeros((SUB * p, 2 * order), jnp.float32)] if p else []

time: 78.2 us -> 78 us (level)
  no operation moved by 1% of the time
where the time goes in v1:
time: 78 us; the launch traced here: 77.8 us
  waiting for transfers between devices  31.1 us (40%)
  starting transfers between devices  27 us (35%)
  Pallas kernels  18.4 us (24%)
  between operations  1 us (1%)
    pallas_call x32, Pallas kernels, call(): pl.pallas_call(kernel, out_shape=outs, in_specs=specs or [VMEM] * len(ins...  18.4 us
    ppermute x8, starting transfers between devices, exchange(): return lax.ppermute(value, 'gx', pairs + [(k, i) for i, k in pairs])  17.2 us
    ppermute x8, waiting for transfers between devices, exchange(): return lax.ppermute(value, 'gx', pairs + [(k, i) for i, k in pairs])  16.9 us
    ppermute x7, starting transfers between devices, butterfly(): lax.ppermute(value, axis, [(i, i ^ move) for i in range(count)])  8.76 us
    ppermute x7, waiting for transfers between devices, butterfly(): lax.ppermute(value, axis, [(i, i ^ move) for i in range(count)])  8.16 us
    ppermute x8, waiting for transfers between devices, along_y(): return [lax.ppermute(value, 'gy', [(0, 1), (1, 0)])]  6.05 us
  transfers between devices with their start and end apart: 23, of which 18 were waited for; matrix products, arithmetic and copies ran while one was open for 0% of the time, Pallas kernels for 14%

profile of v1, /device:TPU:0, one launch (start us, length us, event | category | flops | bytes accessed | tf_op | source)
XLA Modules:
  0.0 77.8 jit_solution(10526364332474652777)
XLA Ops:
  0.7 2.2 %shard_map.94 = (f32[12,32,128]{2,1,0:T(8,128)S(1)}, f32[12,32,128]{2,1,0:T(8,128)S(1)}, f32[17,32,128]{2,1,0:T(8,128)S(1)}, f32[17,32,128]{2,1,0:T(8,128)S(1)},...) custom-call(f32[3,256,128]{2,1,0:T(8,128)} %bitcast.8, f32[2,256,128]{2,1,0:T(8,128)} %bitcast.15, ...), custom_call_target="tpu_custom_call" | custom-call | bytes 2916352 | tf_op jit(solution)/shard_map/pallas_call | solution.py:764
  2.8 3.0 %collective-permute-start.2 = (f32[17,32,128]{2,1,0:T(8,128)S(1)}, f32[17,32,128]{2,1,0:T(8,128)S(1)}, u32[]{:S(2)}, u32[]{:S(2)}) collective-permute-start(f32[17,32,128]{2,1,0:T(8,128)S(1)} %get-tuple-element.71), channel_id=1, source_target_pairs={{0,2},{4,6},{8,10},{12,14},{16,18},{20,22},{24,26},{28,30},{2,0},{... | collective-permute-start | bytes 835592 | tf_op jit(solution)/shard_map/ppermute | solution.py:809
  8.5 9.2 %collective-permute-done.2.refs_1_.halo_ref.first_halo.near_ref.refs_3_.refs_2_ = f32[17,32,128]{2,1,0:T(8,128)S(1)} collective-permute-done((f32[17,32,128]{2,1,0:T(8,128)S(1)}, f32[17,32,128]{2,1,0:T(8,128)S(1)}, u32[]{:S(2)}, u32[]{:S(2)}) %collective-permute-start.2) | collective-permute-done | bytes 278560 | tf_op jit(solution)/shard_map/ppermute | solution.py:809
  19.3 5.0 %collective-permute-start.4 = (f32[12,32,128]{2,1,0:T(8,128)S(1)}, f32[12,32,128]{2,1,0:T(8,128)S(1)}, u32[]{:S(2)}, u32[]{:S(2)}) collective-permute-start(f32[12,32,128]{2,1,0:T(8,128)S(1)} %get-tuple-element.75), channel_id=1, source_target_pairs={{0,2},{4,6},{8,10},{12,14},{16,18},{20,22},{24,26},{28,30},{2,0},{... | collective-permute-start | bytes 589832 | tf_op jit(solution)/shard_map/ppermute | solution.py:809
  24.5 1.2 %collective-permute-done.5.refs_4_.refs_0_ = f32[4,32,128]{2,1,0:T(8,128)S(1)} collective-permute-done((f32[4,32,128]{2,1,0:T(8,128)S(1)}, f32[4,32,128]{2,1,0:T(8,128)S(1)}, u32[]{:S(2)}, u32[]{:S(2)}) %collective-permute-start.5) | collective-permute-done | bytes 65568 | tf_op jit(solution)/shard_map/ppermute | solution.py:813
  29.2 2.8 %collective-permute-done.4.near_ref.halo_ref = f32[12,32,128]{2,1,0:T(8,128)S(1)} collective-permute-done((f32[12,32,128]{2,1,0:T(8,128)S(1)}, f32[12,32,128]{2,1,0:T(8,128)S(1)}, u32[]{:S(2)}, u32[]{:S(2)}) %collective-permute-start.4) | collective-permute-done | bytes 196640 | tf_op jit(solution)/shard_map/ppermute | solution.py:809
  32.5 2.9 %collective-permute-start.11 = (f32[12,32,128]{2,1,0:T(8,128)S(1)}, f32[12,32,128]{2,1,0:T(8,128)S(1)}, u32[]{:S(2)}, u32[]{:S(2)}) collective-permute-start(f32[12,32,128]{2,1,0:T(8,128)S(1)} %get-tuple-element.97), channel_id=1, source_target_pairs={{0,2},{4,6},{8,10},{12,14},{16,18},{20,22},{24,26},{28,30},{2,0},{... | collective-permute-start | bytes 589832 | tf_op jit(solution)/shard_map/ppermute | solution.py:809
  35.5 1.2 %collective-permute-done.7.refs_0_ = f32[2,32,128]{2,1,0:T(8,128)S(1)} collective-permute-done((f32[2,32,128]{2,1,0:T(8,128)S(1)}, f32[2,32,128]{2,1,0:T(8,128)S(1)}, u32[]{:S(2)}, u32[]{:S(2)}) %collective-permute-start.7) | collective-permute-done | bytes 32800 | tf_op jit(solution)/shard_map/ppermute | solution.py:813
  39.5 0.9 %collective-permute-start.10 = (f32[12,32,128]{2,1,0:T(8,128)S(1)}, f32[12,32,128]{2,1,0:T(8,128)S(1)}, u32[]{:S(2)}, u32[]{:S(2)}) collective-permute-start(f32[12,32,128]{2,1,0:T(8,128)S(1)} %get-tuple-element.96), channel_id=1, source_target_pairs={{2,4},{6,8},{10,12},{14,16},{18,20},{22,24},{26,28},{4,2},{8,6},{1... | collective-permute-start | bytes 589832 | tf_op jit(solution)/shard_map/ppermute | solution.py:809
  40.4 1.9 %collective-permute-done.11.halo_ref.near_ref = f32[12,32,128]{2,1,0:T(8,128)S(1)} collective-permute-done((f32[12,32,128]{2,1,0:T(8,128)S(1)}, f32[12,32,128]{2,1,0:T(8,128)S(1)}, u32[]{:S(2)}, u32[]{:S(2)}) %collective-permute-start.11) | collective-permute-done | bytes 196640 | tf_op jit(solution)/shard_map/ppermute | solution.py:809
  42.8 3.5 %collective-permute-start.12 = (f32[12,32,128]{2,1,0:T(8,128)S(1)}, f32[12,32,128]{2,1,0:T(8,128)S(1)}, u32[]{:S(2)}, u32[]{:S(2)}) collective-permute-start(f32[12,32,128]{2,1,0:T(8,128)S(1)} %get-tuple-element.99), channel_id=1, source_target_pairs={{0,2},{4,6},{8,10},{12,14},{16,18},{20,22},{24,26},{28,30},{2,0},{... | collective-permute-start | bytes 589832 | tf_op jit(solution)/shard_map/ppermute | solution.py:809
  46.4 1.2 %collective-permute-done.13.refs_0_ = f32[2,32,128]{2,1,0:T(8,128)S(1)} collective-permute-done((f32[2,32,128]{2,1,0:T(8,128)S(1)}, f32[2,32,128]{2,1,0:T(8,128)S(1)}, u32[]{:S(2)}, u32[]{:S(2)}) %collective-permute-start.13) | collective-permute-done | bytes 32800 | tf_op jit(solution)/shard_map/ppermute | solution.py:813
  50.4 2.9 %collective-permute-done.12.near_ref.halo_ref = f32[12,32,128]{2,1,0:T(8,128)S(1)} collective-permute-done((f32[12,32,128]{2,1,0:T(8,128)S(1)}, f32[12,32,128]{2,1,0:T(8,128)S(1)}, u32[]{:S(2)}, u32[]{:S(2)}) %collective-permute-start.12) | collective-permute-done | bytes 196640 | tf_op jit(solution)/shard_map/ppermute | solution.py:809
  55.5 1.1 %collective-permute-done.16.refs_1_ = f32[192,128]{1,0:T(8,128)S(1)} collective-permute-done((f32[192,128]{1,0:T(8,128)S(1)}, f32[192,128]{1,0:T(8,128)S(1)}, u32[]{:S(2)}, u32[]{:S(2)}) %collective-permute-start.16) | collective-permute-done | bytes 98336 | tf_op jit(solution)/shard_map/ppermute | solution.py:784
  57.1 2.5 %collective-permute-start.17 = (f32[72,128]{1,0:T(8,128)S(1)}, f32[72,128]{1,0:T(8,128)S(1)}, u32[]{:S(2)}, u32[]{:S(2)}) collective-permute-start(f32[72,128]{1,0:T(8,128)S(1)} %get-tuple-element.116), channel_id=1, source_target_pairs={{0,2},{2,0},{4,6},{6,4},{8,10},{10,8},{12,14},{14,12},{16,18},{18,... | collective-permute-start | bytes 110600 | tf_op jit(solution)/shard_map/ppermute | solution.py:784
  59.6 1.5 %collective-permute-start.19 = (f32[72,128]{1,0:T(8,128)S(1)}, f32[72,128]{1,0:T(8,128)S(1)}, u32[]{:S(2)}, u32[]{:S(2)}) collective-permute-start(f32[72,128]{1,0:T(8,128)S(1)} %get-tuple-element.116), channel_id=1, source_target_pairs={{0,6},{2,4},{4,2},{6,0},{8,14},{10,12},{12,10},{14,8},{16,22},{18,... | collective-permute-start | bytes 110600 | tf_op jit(solution)/shard_map/ppermute | solution.py:784
  61.5 2.2 %collective-permute-done.18 = f32[72,128]{1,0:T(8,128)S(1)} collective-permute-done((f32[72,128]{1,0:T(8,128)S(1)}, f32[72,128]{1,0:T(8,128)S(1)}, u32[]{:S(2)}, u32[]{:S(2)}) %collective-permute-start.18) | collective-permute-done | bytes 36896 | tf_op jit(solution)/shard_map/ppermute | solution.py:784
  64.5 1.8 %collective-permute-start.20 = (f32[72,128]{1,0:T(8,128)S(1)}, f32[72,128]{1,0:T(8,128)S(1)}, u32[]{:S(2)}, u32[]{:S(2)}) collective-permute-start(f32[72,128]{1,0:T(8,128)S(1)} %add_add_fusion.refs_0_), channel_id=1, source_target_pairs={{0,8},{2,10},{4,12},{6,14},{8,0},{10,2},{12,4},{14,6},{16,24},{18,... | collective-permute-start | bytes 110600 | tf_op jit(solution)/shard_map/ppermute | solution.py:784
  66.3 1.6 %collective-permute-start.21 = (f32[72,128]{1,0:T(8,128)S(1)}, f32[72,128]{1,0:T(8,128)S(1)}, u32[]{:S(2)}, u32[]{:S(2)}) collective-permute-start(f32[72,128]{1,0:T(8,128)S(1)} %add_add_fusion.refs_0_), channel_id=1, source_target_pairs={{0,16},{2,18},{4,20},{6,22},{8,24},{10,26},{12,28},{14,30},{16,0},... | collective-permute-start | bytes 110600 | tf_op jit(solution)/shard_map/ppermute | solution.py:784
  67.8 1.1 %collective-permute-start.22 = (f32[72,128]{1,0:T(8,128)S(1)}, f32[72,128]{1,0:T(8,128)S(1)}, u32[]{:S(2)}, u32[]{:S(2)}) collective-permute-start(f32[72,128]{1,0:T(8,128)S(1)} %add_add_fusion.refs_0_), channel_id=1, source_target_pairs={{0,24},{2,26},{4,28},{6,30},{8,16},{10,18},{12,20},{14,22},{16,8},... | collective-permute-start | bytes 110600 | tf_op jit(solution)/shard_map/ppermute | solution.py:784
  68.9 1.0 %shard_map.122 = f32[3,256,128]{2,1,0:T(8,128)} custom-call(f32[12,32,128]{2,1,0:T(8,128)S(1)} %get-tuple-element.113.far_ref.refs_0_, f32[12,32,128]{2,1,0:T(8,128)S(1)} %get-tuple-element.114.near_ref.refs_1_), custom_call_target="tpu_custom_call" | custom-call | bytes 786432 | tf_op jit(solution)/shard_map/pallas_call | solution.py:764
  69.9 1.9 %collective-permute-done.21.refs_2_ = f32[72,128]{1,0:T(8,128)S(1)} collective-permute-done((f32[72,128]{1,0:T(8,128)S(1)}, f32[72,128]{1,0:T(8,128)S(1)}, u32[]{:S(2)}, u32[]{:S(2)}) %collective-permute-start.21) | collective-permute-done | bytes 36896 | tf_op jit(solution)/shard_map/ppermute | solution.py:784
  71.8 1.8 %collective-permute-done.22.refs_3_ = f32[72,128]{1,0:T(8,128)S(1)} collective-permute-done((f32[72,128]{1,0:T(8,128)S(1)}, f32[72,128]{1,0:T(8,128)S(1)}, u32[]{:S(2)}, u32[]{:S(2)}) %collective-permute-start.22) | collective-permute-done | bytes 36896 | tf_op jit(solution)/shard_map/ppermute | solution.py:784
  73.6 4.2 %shard_map.125 = (f32[4,24,128]{2,1,0:T(8,128)}, f32[128,128]{1,0:T(8,128)}) custom-call(f32[4,48,128]{2,1,0:T(8,128)S(1)} %bitcast.13, f32[72,128]{1,0:T(8,128)S(1)} %add_add_fusion.refs_0_, f32[72,128]{1,0:T(8,128)S(1)} %collective-permute-done.20.refs_1_, f32[72,128]{1,0:T(8,128)S(1)} %collective-permute-done.21.refs_2_, ...), custom_call_target="tpu_custom_call" | custom-call | bytes 360448 | tf_op jit(solution)/shard_map/pallas_call | solution.py:764
  (63 shorter events, 18.2 us)
Async XLA Ops:
  0.6 6.0 %copy-start.1 = (f32[3,32,8,128]{3,2,1,0:T(8,128)S(1)}, f32[3,32,8,128]{3,2,1,0:T(8,128)}, u32[]{:S(2)}) copy-start(f32[3,32,8,128]{3,2,1,0:T(8,128)} %param.7) | copy-start | bytes 1179652
  2.8 14.9 %collective-permute-start.2 = (f32[17,32,128]{2,1,0:T(8,128)S(1)}, f32[17,32,128]{2,1,0:T(8,128)S(1)}, u32[]{:S(2)}, u32[]{:S(2)}) collective-permute-start(f32[17,32,128]{2,1,0:T(8,128)S(1)} %get-tuple-element.71), channel_id=1, source_target_pairs={{0,2},{4,6},{8,10},{12,14},{16,18},{20,22},{24,26},{28,30},{2,0},{... | collective-permute-start | bytes 835592 | tf_op jit(solution)/shard_map/ppermute | solution.py:809
  5.9 11.9 %collective-permute-start = (f32[17,32,128]{2,1,0:T(8,128)S(1)}, f32[17,32,128]{2,1,0:T(8,128)S(1)}, u32[]{:S(2)}, u32[]{:S(2)}) collective-permute-start(f32[17,32,128]{2,1,0:T(8,128)S(1)} %get-tuple-element.63), channel_id=1, source_target_pairs={{2,4},{6,8},{10,12},{14,16},{18,20},{22,24},{26,28},{4,2},{8,6},{1... | collective-permute-start | bytes 835592 | tf_op jit(solution)/shard_map/ppermute | solution.py:809
  6.5 1.4 %collective-permute-start.1 = (f32[8,32,128]{2,1,0:T(8,128)S(1)}, f32[8,32,128]{2,1,0:T(8,128)S(1)}, u32[]{:S(2)}, u32[]{:S(2)}) collective-permute-start(f32[8,32,128]{2,1,0:T(8,128)S(1)} %get-tuple-element.67.refs_2_.refs_5_.edge_ref), channel_id=1, source_target_pairs={{0,1},{1,0},{2,3},{3,2},{4,5},{5,4},{6,7},{7,6},{8,9},{9,8},{10,11... | collective-permute-start | bytes 393224 | tf_op jit(solution)/shard_map/ppermute | solution.py:813
  18.2 9.9 %collective-permute-start.3 = (f32[12,32,128]{2,1,0:T(8,128)S(1)}, f32[12,32,128]{2,1,0:T(8,128)S(1)}, u32[]{:S(2)}, u32[]{:S(2)}) collective-permute-start(f32[12,32,128]{2,1,0:T(8,128)S(1)} %get-tuple-element.72), channel_id=1, source_target_pairs={{2,4},{6,8},{10,12},{14,16},{18,20},{22,24},{26,28},{4,2},{8,6},{1... | collective-permute-start | bytes 589832 | tf_op jit(solution)/shard_map/ppermute | solution.py:809
  19.3 12.7 %collective-permute-start.4 = (f32[12,32,128]{2,1,0:T(8,128)S(1)}, f32[12,32,128]{2,1,0:T(8,128)S(1)}, u32[]{:S(2)}, u32[]{:S(2)}) collective-permute-start(f32[12,32,128]{2,1,0:T(8,128)S(1)} %get-tuple-element.75), channel_id=1, source_target_pairs={{0,2},{4,6},{8,10},{12,14},{16,18},{20,22},{24,26},{28,30},{2,0},{... | collective-permute-start | bytes 589832 | tf_op jit(solution)/shard_map/ppermute | solution.py:809
  24.4 1.3 %collective-permute-start.5 = (f32[4,32,128]{2,1,0:T(8,128)S(1)}, f32[4,32,128]{2,1,0:T(8,128)S(1)}, u32[]{:S(2)}, u32[]{:S(2)}) collective-permute-start(f32[4,32,128]{2,1,0:T(8,128)S(1)} %shard_map.99), channel_id=1, source_target_pairs={{0,1},{1,0},{2,3},{3,2},{4,5},{5,4},{6,7},{7,6},{8,9},{9,8},{10,11... | collective-permute-start | bytes 196616 | tf_op jit(solution)/shard_map/ppermute | solution.py:813
  26.2 1.3 %collective-permute-start.6 = (f32[3,32,128]{2,1,0:T(8,128)S(1)}, f32[3,32,128]{2,1,0:T(8,128)S(1)}, u32[]{:S(2)}, u32[]{:S(2)}) collective-permute-start(f32[3,32,128]{2,1,0:T(8,128)S(1)} %get-tuple-element.81.refs_2_.edge_ref), channel_id=1, source_target_pairs={{0,1},{1,0},{2,3},{3,2},{4,5},{5,4},{6,7},{7,6},{8,9},{9,8},{10,11... | collective-permute-start | bytes 147464 | tf_op jit(solution)/shard_map/ppermute | solution.py:813
  28.6 10.5 %collective-permute-start.8 = (f32[12,32,128]{2,1,0:T(8,128)S(1)}, f32[12,32,128]{2,1,0:T(8,128)S(1)}, u32[]{:S(2)}, u32[]{:S(2)}) collective-permute-start(f32[12,32,128]{2,1,0:T(8,128)S(1)} %get-tuple-element.91), channel_id=1, source_target_pairs={{2,4},{6,8},{10,12},{14,16},{18,20},{22,24},{26,28},{4,2},{8,6},{1... | collective-permute-start | bytes 589832 | tf_op jit(solution)/shard_map/ppermute | solution.py:809
  32.5 9.8 %collective-permute-start.11 = (f32[12,32,128]{2,1,0:T(8,128)S(1)}, f32[12,32,128]{2,1,0:T(8,128)S(1)}, u32[]{:S(2)}, u32[]{:S(2)}) collective-permute-start(f32[12,32,128]{2,1,0:T(8,128)S(1)} %get-tuple-element.97), channel_id=1, source_target_pairs={{0,2},{4,6},{8,10},{12,14},{16,18},{20,22},{24,26},{28,30},{2,0},{... | collective-permute-start | bytes 589832 | tf_op jit(solution)/shard_map/ppermute | solution.py:809
  35.5 1.3 %collective-permute-start.7 = (f32[2,32,128]{2,1,0:T(8,128)S(1)}, f32[2,32,128]{2,1,0:T(8,128)S(1)}, u32[]{:S(2)}, u32[]{:S(2)}) collective-permute-start(f32[2,32,128]{2,1,0:T(8,128)S(1)} %shard_map.105), channel_id=1, source_target_pairs={{0,1},{1,0},{2,3},{3,2},{4,5},{5,4},{6,7},{7,6},{8,9},{9,8},{10,11... | collective-permute-start | bytes 98312 | tf_op jit(solution)/shard_map/ppermute | solution.py:813
  37.2 1.3 %collective-permute-start.9 = (f32[3,32,128]{2,1,0:T(8,128)S(1)}, f32[3,32,128]{2,1,0:T(8,128)S(1)}, u32[]{:S(2)}, u32[]{:S(2)}) collective-permute-start(f32[3,32,128]{2,1,0:T(8,128)S(1)} %get-tuple-element.92.refs_2_.edge_ref), channel_id=1, source_target_pairs={{0,1},{1,0},{2,3},{3,2},{4,5},{5,4},{6,7},{7,6},{8,9},{9,8},{10,11... | collective-permute-start | bytes 147464 | tf_op jit(solution)/shard_map/ppermute | solution.py:813
  39.5 10.4 %collective-permute-start.10 = (f32[12,32,128]{2,1,0:T(8,128)S(1)}, f32[12,32,128]{2,1,0:T(8,128)S(1)}, u32[]{:S(2)}, u32[]{:S(2)}) collective-permute-start(f32[12,32,128]{2,1,0:T(8,128)S(1)} %get-tuple-element.96), channel_id=1, source_target_pairs={{2,4},{6,8},{10,12},{14,16},{18,20},{22,24},{26,28},{4,2},{8,6},{1... | collective-permute-start | bytes 589832 | tf_op jit(solution)/shard_map/ppermute | solution.py:809
  42.8 10.5 %collective-permute-start.12 = (f32[12,32,128]{2,1,0:T(8,128)S(1)}, f32[12,32,128]{2,1,0:T(8,128)S(1)}, u32[]{:S(2)}, u32[]{:S(2)}) collective-permute-start(f32[12,32,128]{2,1,0:T(8,128)S(1)} %get-tuple-element.99), channel_id=1, source_target_pairs={{0,2},{4,6},{8,10},{12,14},{16,18},{20,22},{24,26},{28,30},{2,0},{... | collective-permute-start | bytes 589832 | tf_op jit(solution)/shard_map/ppermute | solution.py:809
  46.3 1.3 %collective-permute-start.13 = (f32[2,32,128]{2,1,0:T(8,128)S(1)}, f32[2,32,128]{2,1,0:T(8,128)S(1)}, u32[]{:S(2)}, u32[]{:S(2)}) collective-permute-start(f32[2,32,128]{2,1,0:T(8,128)S(1)} %shard_map.114), channel_id=1, source_target_pairs={{0,1},{1,0},{2,3},{3,2},{4,5},{5,4},{6,7},{7,6},{8,9},{9,8},{10,11... | collective-permute-start | bytes 98312 | tf_op jit(solution)/shard_map/ppermute | solution.py:813
  48.1 1.3 %collective-permute-start.14 = (f32[3,32,128]{2,1,0:T(8,128)S(1)}, f32[3,32,128]{2,1,0:T(8,128)S(1)}, u32[]{:S(2)}, u32[]{:S(2)}) collective-permute-start(f32[3,32,128]{2,1,0:T(8,128)S(1)} %get-tuple-element.105.refs_2_), channel_id=1, source_target_pairs={{0,1},{1,0},{2,3},{3,2},{4,5},{5,4},{6,7},{7,6},{8,9},{9,8},{10,11... | collective-permute-start | bytes 147464 | tf_op jit(solution)/shard_map/ppermute | solution.py:813
  53.4 1.3 %collective-permute-start.15 = (f32[2,32,128]{2,1,0:T(8,128)S(1)}, f32[2,32,128]{2,1,0:T(8,128)S(1)}, u32[]{:S(2)}, u32[]{:S(2)}) collective-permute-start(f32[2,32,128]{2,1,0:T(8,128)S(1)} %shard_map.119), channel_id=1, source_target_pairs={{0,1},{1,0},{2,3},{3,2},{4,5},{5,4},{6,7},{7,6},{8,9},{9,8},{10,11... | collective-permute-start | bytes 98312 | tf_op jit(solution)/shard_map/ppermute | solution.py:813
  55.3 1.4 %collective-permute-start.16 = (f32[192,128]{1,0:T(8,128)S(1)}, f32[192,128]{1,0:T(8,128)S(1)}, u32[]{:S(2)}, u32[]{:S(2)}) collective-permute-start(f32[192,128]{1,0:T(8,128)S(1)} %shard_map.123.refs_0_), channel_id=1, source_target_pairs={{0,1},{1,0},{2,3},{3,2},{4,5},{5,4},{6,7},{7,6},{8,9},{9,8},{10,11... | collective-permute-start | bytes 294920 | tf_op jit(solution)/shard_map/ppermute | solution.py:784
  57.1 4.5 %collective-permute-start.17 = (f32[72,128]{1,0:T(8,128)S(1)}, f32[72,128]{1,0:T(8,128)S(1)}, u32[]{:S(2)}, u32[]{:S(2)}) collective-permute-start(f32[72,128]{1,0:T(8,128)S(1)} %get-tuple-element.116), channel_id=1, source_target_pairs={{0,2},{2,0},{4,6},{6,4},{8,10},{10,8},{12,14},{14,12},{16,18},{18,... | collective-permute-start | bytes 110600 | tf_op jit(solution)/shard_map/ppermute | solution.py:784
  59.6 4.2 %collective-permute-start.18 = (f32[72,128]{1,0:T(8,128)S(1)}, f32[72,128]{1,0:T(8,128)S(1)}, u32[]{:S(2)}, u32[]{:S(2)}) collective-permute-start(f32[72,128]{1,0:T(8,128)S(1)} %get-tuple-element.116), channel_id=1, source_target_pairs={{0,4},{2,6},{4,0},{6,2},{8,12},{10,14},{12,8},{14,10},{16,20},{18,... | collective-permute-start | bytes 110600 | tf_op jit(solution)/shard_map/ppermute | solution.py:784
  59.6 4.9 %collective-permute-start.19 = (f32[72,128]{1,0:T(8,128)S(1)}, f32[72,128]{1,0:T(8,128)S(1)}, u32[]{:S(2)}, u32[]{:S(2)}) collective-permute-start(f32[72,128]{1,0:T(8,128)S(1)} %get-tuple-element.116), channel_id=1, source_target_pairs={{0,6},{2,4},{4,2},{6,0},{8,14},{10,12},{12,10},{14,8},{16,22},{18,... | collective-permute-start | bytes 110600 | tf_op jit(solution)/shard_map/ppermute | solution.py:784
  64.5 5.4 %collective-permute-start.20 = (f32[72,128]{1,0:T(8,128)S(1)}, f32[72,128]{1,0:T(8,128)S(1)}, u32[]{:S(2)}, u32[]{:S(2)}) collective-permute-start(f32[72,128]{1,0:T(8,128)S(1)} %add_add_fusion.refs_0_), channel_id=1, source_target_pairs={{0,8},{2,10},{4,12},{6,14},{8,0},{10,2},{12,4},{14,6},{16,24},{18,... | collective-permute-start | bytes 110600 | tf_op jit(solution)/shard_map/ppermute | solution.py:784
  66.3 5.5 %collective-permute-start.21 = (f32[72,128]{1,0:T(8,128)S(1)}, f32[72,128]{1,0:T(8,128)S(1)}, u32[]{:S(2)}, u32[]{:S(2)}) collective-permute-start(f32[72,128]{1,0:T(8,128)S(1)} %add_add_fusion.refs_0_), channel_id=1, source_target_pairs={{0,16},{2,18},{4,20},{6,22},{8,24},{10,26},{12,28},{14,30},{16,0},... | collective-permute-start | bytes 110600 | tf_op jit(solution)/shard_map/ppermute | solution.py:784
  67.8 5.8 %collective-permute-start.22 = (f32[72,128]{1,0:T(8,128)S(1)}, f32[72,128]{1,0:T(8,128)S(1)}, u32[]{:S(2)}, u32[]{:S(2)}) collective-permute-start(f32[72,128]{1,0:T(8,128)S(1)} %add_add_fusion.refs_0_), channel_id=1, source_target_pairs={{0,24},{2,26},{4,28},{6,30},{8,16},{10,18},{12,20},{14,22},{16,8},... | collective-permute-start | bytes 110600 | tf_op jit(solution)/shard_map/ppermute | solution.py:784
  (3 other events, 12.9 us)
